TPU v7x, 32 devices: a whole 2x2x4 slice. The times are simulated.
32 devices in a mesh: tile: 8 (over z, y), row: 4 (over x, core).
Axes of the slice: x: 2, y: 2, z: 4, core: 2. Of those that a mesh axis runs over, the one named last changes fastest.
Arguments:
- intensity: bfloat16 [8, 128, 11264], P('tile', 'row'), may hold values from 0.099609375 to 1
- volume: float32 [64, 128, 256], P('tile', 'row'), may hold values from 0 to 1
- footprint: bfloat16 [8, 256, 256], P('tile'), may hold values from 0.0010681152 to 0.021484375
- foot_offset: int32 [64, 8], replicated, may hold values from 2 to 84, as said below
- tile_count: int32 [8], replicated, may hold values from 1 to 8, as said below
Outputs:
- residual: float32 [8, 128, 11264], P('tile', 'row')
- correction: float32 [64, 128, 256], P('tile', 'row')
Inputs may be any that keep to these rules, and one draw needn't show every extreme that they name: `foot_offset`: slot j belongs to group j // 8. At every angle the offsets of one group's slots differ by at most 3; wherever a group has two or more slots, by exactly 3. `tile_count`: some group has all its slots live.
All inputs are finite; a program needn't handle non-finite values.
Results may differ from a plain program's by a relative error of at most 0.00065.
Values may be sent and summed in bfloat16 or wider, within the bound.
No kernel may reach another device: no remote copies, remote signals or barrier semaphores. Data moves between devices by JAX's collectives and lax.ppermute only.
A program may use at most 128 MiB of HBM per device.

v0:
```python
import jax
import jax.numpy as jnp
import numpy as np
from jax import lax
from jax.sharding import PartitionSpec as P

SPREAD = 4
RIM = 3
decay_length = 2.0
row_floor = 0.5


def with_halo(block, sides, width):
    for axis, dim in sides:
        count = lax.axis_size(axis)
        forward = [(i, i + 1) for i in range(count - 1)]
        backward = [(target, source) for source, target in forward]
        low = lax.ppermute(
            lax.slice_in_dim(block, block.shape[dim] - width, None, axis=dim), axis, forward
        )
        high = lax.ppermute(lax.slice_in_dim(block, 0, width, axis=dim), axis, backward)
        block = jnp.concatenate([low, block, high], axis=dim)
    return block


def smoothing_taps():
    spread_taps = np.exp(-np.abs(np.arange(-RIM, RIM + 1)) / decay_length)
    return spread_taps / spread_taps.sum()


def retrieve_phase(intensity):
    padded = with_halo(intensity, (("row", 1),), RIM)
    tap_weights = smoothing_taps()
    height_rows = intensity.shape[1]
    column_count = intensity.shape[2]
    across = float(tap_weights[0]) * padded[:, 0:height_rows, :].astype(jnp.float32)
    for tap_index in range(1, 2 * RIM + 1):
        across = across + float(tap_weights[tap_index]) * padded[
            :, tap_index : tap_index + height_rows, :
        ].astype(jnp.float32)
    widened = jnp.pad(across, ((0, 0), (0, 0), (RIM, RIM)))
    smoothed = float(tap_weights[0]) * widened[:, :, 0:column_count]
    for tap_index in range(1, 2 * RIM + 1):
        smoothed = (
            smoothed
            + float(tap_weights[tap_index]) * widened[:, :, tap_index : tap_index + column_count]
        )
    return -jnp.log(smoothed)


def live_flags(tile_count, slots_here):
    group_total = tile_count.shape[0]
    slot_ids = jnp.arange(group_total * slots_here, dtype=jnp.int32)
    repeated = jnp.broadcast_to(tile_count[:, None], (group_total, slots_here)).reshape(-1)
    return (slot_ids % slots_here < repeated).astype(jnp.float32)


def row_totals(footprint, offsets_here, live_all, block_count):
    half_cols = footprint.shape[2] // 2
    block_ids = jnp.arange(block_count, dtype=jnp.int32)
    matches = (offsets_here[:, :, None] == block_ids[None, None, :]).astype(jnp.float32)
    counts = jnp.sum(matches * live_all[:, None, None], axis=0)
    voxel_sums = jnp.sum(footprint, axis=1, dtype=jnp.float32)
    leading = counts[:, :, None] * voxel_sums[:, None, :half_cols]
    trailing = counts[:, :, None] * voxel_sums[:, None, half_cols:]
    trailing = jnp.concatenate([jnp.zeros_like(trailing[:, :1]), trailing[:, :-1]], axis=1)
    return (leading + trailing).reshape(counts.shape[0], -1)


def project_loads(load_half, footprint):
    half_cols = footprint.shape[2] // 2
    images = jnp.einsum("abrv,avc->arbc", load_half, footprint, preferred_element_type=jnp.float32)
    leading = images[..., :half_cols]
    trailing = images[..., half_cols:]
    trailing = jnp.concatenate([jnp.zeros_like(trailing[:, :, :1]), trailing[:, :, :-1]], axis=2)
    joined = leading + trailing
    return joined.reshape(joined.shape[0], joined.shape[1], -1)


def back_project(weighted, footprint):
    half_cols = footprint.shape[2] // 2
    halves = weighted.reshape(weighted.shape[0], weighted.shape[1], -1, half_cols)
    nearer = jnp.einsum(
        "arbc,avc->abrv", halves, footprint[:, :, :half_cols], preferred_element_type=jnp.float32
    )
    farther = jnp.einsum(
        "arbc,avc->abrv", halves, footprint[:, :, half_cols:], preferred_element_type=jnp.float32
    )
    farther = jnp.concatenate([farther[:, 1:], jnp.zeros_like(farther[:, :1])], axis=1)
    return nearer + farther


def local(intensity, volume, footprint, foot_offset, tile_count):
    phase_map = retrieve_phase(intensity)
    slots_here = volume.shape[0]
    angles_here = footprint.shape[0]
    half_cols = footprint.shape[2] // 2
    block_count = intensity.shape[2] // half_cols
    member = lax.axis_index("tile")
    live_all = live_flags(tile_count, slots_here)
    live_mine = lax.dynamic_slice_in_dim(live_all, member * slots_here, slots_here)
    masked = volume * live_mine[:, None, None]
    offsets_here = lax.dynamic_slice_in_dim(foot_offset, member * angles_here, angles_here, 1)
    column_sums = lax.psum(jnp.sum(footprint, axis=(0, 2), dtype=jnp.float32), "tile")
    row_sums = row_totals(footprint, offsets_here, live_all, block_count)
    group_total = tile_count.shape[0]
    grouped = foot_offset.reshape(group_total, slots_here, -1)
    starts = jnp.min(grouped, axis=1)
    deltas = lax.dynamic_slice_in_dim(grouped, member, 1, 0)[0] - lax.dynamic_slice_in_dim(
        starts, member, 1, 0
    )
    places = jnp.arange(SPREAD, dtype=jnp.int32)
    picked = (deltas[:, :, None] == places[None, None, :]).astype(jnp.float32)
    outgoing = jnp.einsum("jas,jrv->asrv", picked, masked, precision=lax.Precision.HIGHEST)
    arrived = lax.all_to_all(
        outgoing.astype(jnp.bfloat16), "tile", split_axis=0, concat_axis=1, tiled=True
    ).astype(outgoing.dtype)
    starts_here = lax.dynamic_slice_in_dim(starts, member * angles_here, angles_here, 1)
    targets = (jnp.transpose(starts_here)[:, :, None] + places[None, None, :]).reshape(
        angles_here, -1
    )
    load_blocks = jnp.stack([jax.ops.segment_sum(arrived[0], targets[0], num_segments=block_count)])
    projection = project_loads(load_blocks.astype(jnp.bfloat16), footprint)
    residual = phase_map - projection
    weighted = (residual / jnp.maximum(row_sums, row_floor)[:, None, :]).astype(jnp.bfloat16)
    back_blocks = back_project(weighted, footprint)
    returned = jnp.stack([jnp.take(back_blocks[0], targets[0], axis=0)])
    received = lax.all_to_all(returned, "tile", split_axis=1, concat_axis=0, tiled=True)
    summed = jnp.einsum("jas,asrv->jrv", picked, received, precision=lax.Precision.HIGHEST)
    correction = summed * live_mine[:, None, None] / column_sums[None, None, :]
    return (residual, correction)


def solution(mesh):
    placed = (P("tile", "row", None), P("tile", "row", None), P("tile", None, None), P(), P())
    return jax.shard_map(
        local,
        mesh=mesh,
        in_specs=placed,
        out_specs=(P("tile", "row", None), P("tile", "row", None)),
        check_vma=False,
    )
```

profile of v0, /device:TPU:8, one launch (start us, length us, event | category | flops | bytes accessed | tf_op | source)
XLA Modules:
  0.0 82.8 jit_solution(16312274930662407107)
XLA Ops:
  0.6 0.7 broadcast_in_dim.12
  1.4 0.1 reshape.331
  1.4 0.8 copy.69
  2.2 0.1 dynamic_slice.23
  2.3 0.0 copy-start.1
  2.3 1.7 %convolution_convert_fusion = bf16[8,4,32,256]{3,0,2,1:T(8,128)(2,1)S(1)} fusion(f32[8,32,256]{2,1,0:T(8,128)} %param.6, f32[8]{0:T(128)S(1)} %dynamic_slice.23, s32[8,8]{1,0:T(8,128)S(1)} %bitcast_subtract_fusion), kind=kOutput, calls=%fused_computation.16 | convolution fusion | flops 25493760 | bytes 786720 | tf_op jit(solution)/shard_map/jas,jrv->asrv/dot_general | solution.py:114
  4.0 0.9 %copy.72 = bf16[8,4,32,256]{3,2,1,0:T(8,128)(2,1)} copy(bf16[8,4,32,256]{3,0,2,1:T(8,128)(2,1)S(1)} %convolution_convert_fusion) | data formatting | bytes 1048576 | tf_op jit(solution)/shard_map/convert_element_type | solution.py:116
  4.9 0.0 copy-start.2
  4.9 6.4 %all-to-all-start = ((bf16[8,4,32,256]{3,2,1,0:T(8,128)(2,1)}), bf16[8,4,32,256]{3,2,1,0:T(8,128)(2,1)S(1)}, u32[]{:S(2)}, u32[]{:S(2)}) async-start(bf16[8,4,32,256]{3,2,1,0:T(8,128)(2,1)} %copy.72), calls=%async_computation | async-start | bytes 1048576 | tf_op jit(solution)/shard_map/all_to_all | solution.py:115
  11.3 0.0 copy-done.1
  11.3 0.1 fusion.28
  11.4 1.3 %collective-permute-start = (bf16[1,3,11264]{2,1,0:T(4,128)(2,1)S(1)}, bf16[1,3,11264]{2,1,0:T(4,128)(2,1)S(1)}, u32[]{:S(2)}, u32[]{:S(2)}) collective-permute-start(bf16[1,3,11264]{2,1,0:T(4,128)(2,1)S(1)} %get-tuple-element.19), channel_id=1, source_target_pairs={{0,1},{1,2},{2,3},{4,5},{5,6},{6,7},{8,9},{9,10},{10,11},{12,13},{... | collective-permute-start | bytes 202760 | tf_op jit(solution)/shard_map/ppermute | solution.py:18
  12.7 1.3 %collective-permute-start.1 = (bf16[1,3,11264]{2,1,0:T(4,128)(2,1)S(1)}, bf16[1,3,11264]{2,1,0:T(4,128)(2,1)S(1)}, u32[]{:S(2)}, u32[]{:S(2)}) collective-permute-start(bf16[1,3,11264]{2,1,0:T(4,128)(2,1)S(1)} %get-tuple-element.18), channel_id=1, source_target_pairs={{1,0},{2,1},{3,2},{5,4},{6,5},{7,6},{9,8},{10,9},{11,10},{13,12},{... | collective-permute-start | bytes 202760 | tf_op jit(solution)/shard_map/ppermute | solution.py:21
  14.0 0.7 fusion.26
  14.7 0.2 dynamic-slice_reduce_fusion
  14.9 0.1 add.151
  15.0 0.1 add.152
  15.1 0.1 add.159
  15.2 0.0 copy-done.2
  15.2 0.1 convert_reduce_fusion
  15.3 0.1 select_reduce_fusion
  15.4 0.1 add.154
  15.5 0.1 add.161
  15.6 0.1 broadcast_multiply_fusion
  15.7 0.1 maximum_bitcast_fusion
  15.8 1.8 %collective-permute-done.1 = bf16[1,3,11264]{2,1,0:T(4,128)(2,1)S(1)} collective-permute-done((bf16[1,3,11264]{2,1,0:T(4,128)(2,1)S(1)}, bf16[1,3,11264]{2,1,0:T(4,128)(2,1)S(1)}, u32[]{:S(2)}, u32[]{:S(2)}) %collective-permute-start.1) | collective-permute-done | bytes 67616 | tf_op jit(solution)/shard_map/ppermute | solution.py:21
  17.6 0.1 constant_dynamic-update-slice_fusion
  17.7 0.0 collective-permute-done
  17.7 2.5 %multiply_add_fusion = f32[1,32,11264]{2,1,0:T(8,128)} fusion(bf16[1,32,11264]{2,1,0:T(8,128)(2,1)S(1)} %copy-done.1, bf16[1,3,11264]{2,1,0:T(4,128)(2,1)S(1)} %collective-permute-done, bf16[1,35,11264]{2,1,0:T(8,128)(2,1)S(1)} %constant_dynamic-update-slice_fusion), kind=kLoop, calls=%fused_computation.15 | loop fusion | flops 10452992 | bytes 4392960 | tf_op jit(solution)/shard_map/add | solution.py:38
  20.2 4.4 %all-to-all-done = bf16[8,4,32,256]{3,2,1,0:T(8,128)(2,1)S(1)} async-done(((bf16[8,4,32,256]{3,2,1,0:T(8,128)(2,1)}), bf16[8,4,32,256]{3,2,1,0:T(8,128)(2,1)S(1)}, u32[]{:S(2)}, u32[]{:S(2)}) %all-to-all-start) | async-done | bytes 524320 | tf_op jit(solution)/shard_map/all_to_all | solution.py:115
  24.6 1.1 %bitcast_convert_fusion = f32[32,32,256]{2,1,0:T(8,128)} fusion(bf16[8,4,32,256]{3,2,1,0:T(8,128)(2,1)S(1)} %all-to-all-done), kind=kLoop, calls=%fused_computation.31 | loop fusion | flops 262144 | bytes 1572864 | tf_op jit(solution)/shard_map/convert_element_type | solution.py:117
  25.7 0.3 broadcast_in_dim.11
  26.0 3.8 %scatter_fusion = f32[88,32,256]{2,1,0:T(8,128)S(1)} fusion(f32[88,32,256]{2,1,0:T(8,128)S(1)} %broadcast_in_dim.11, s32[32]{0:T(128)S(1)} %get-tuple-element.21, f32[32,32,256]{2,1,0:T(8,128)} %bitcast_convert_fusion), kind=kCustom, calls=%fused_computation.1 | custom fusion | flops 262144 | bytes 3145856 | tf_op jit(solution)/shard_map/scatter-add | solution.py:122
  29.8 0.5 convolution_bitcast_fusion.1
  30.4 0.1 slice.107
  30.5 0.2 slice_add_fusion
  30.7 0.0 copy-start
  30.8 0.8 %copy.73 = f32[1,32,88,128]{3,2,0,1:T(8,128)S(1)} copy(f32[1,32,88,128]{3,1,2,0:T(8,128)S(1)} %slice_add_fusion) | data formatting | bytes 2883584 | tf_op jit(solution)/shard_map/add | solution.py:76
  31.6 0.5 copy-done
  32.1 3.4 %fusion.11 = (bf16[4,8,88,128]{3,1,2,0:T(8,128)(2,1)S(1)}, f32[1,32,11264]{2,1,0:T(8,128)}) fusion(f32[11264]{0:T(1024)S(1)} %maximum_bitcast_fusion, f32[1,32,11264]{2,0,1:T(1,128)S(1)} %bitcast.95, f32[1,32,11264]{2,1,0:T(8,128)S(1)} %copy-done), kind=kLoop, calls=%fused_computation.30 | loop fusion | flops 6127616 | bytes 5091328
  35.5 0.1 copy.83
  35.6 0.6 convolution_bitcast_fusion
  36.2 0.2 slice.111
  36.4 0.6 fusion
  37.0 0.9 %copy.75 = f32[88,32,256]{2,1,0:T(8,128)S(1)} copy(f32[88,32,256]{2,0,1:T(8,128)S(1)} %fusion) | data formatting | bytes 5767168 | tf_op jit(solution)/shard_map/squeeze | solution.py:127
  37.9 1.6 %gather_fusion = f32[32,32,256]{2,1,0:T(8,128)} fusion(f32[88,32,256]{2,1,0:T(8,128)S(1)} %copy.75, s32[1024]{0:T(1024)S(1)} %pad_clamp_fusion), kind=kCustom, calls=%fused_computation | custom fusion | bytes 2097280 | tf_op jit(solution)/shard_map/jit(_take)/gather | solution.py:127
  39.5 2.4 %fusion.7 = f32[1,32,32,256]{3,2,0,1:T(8,128)} fusion(f32[32,32,256]{2,1,0:T(8,128)} %gather_fusion, pred[32]{0:T(512)(128)(4,1)S(1)} %compare_and_fusion), kind=kLoop, calls=%fused_computation.23 | loop fusion | flops 262144 | bytes 2097184 | tf_op jit(solution)/shard_map/jit(_take)/select_n | solution.py:127
  41.9 4.9 %all-to-all-start.1 = ((f32[1,32,32,256]{3,2,0,1:T(8,128)}), f32[1,32,32,256]{3,2,0,1:T(8,128)S(1)}, u32[]{:S(2)}, u32[]{:S(2)}) async-start(f32[1,32,32,256]{3,2,0,1:T(8,128)} %fusion.7), calls=%async_computation.1 | async-start | bytes 2097152 | tf_op jit(solution)/shard_map/all_to_all | solution.py:128
  46.8 33.8 %psum.7 = f32[256]{0:T(256)S(1)} all-reduce(f32[256]{0:T(256)S(1)} %get-tuple-element.14), channel_id=1, replica_groups=mesh['tile'=8,'row'=4] {'tile'}, use_global_device_ids=true, to_apply=%region_5.6 | all-reduce | flops 256 | bytes 2048 | tf_op jit(solution)/shard_map/psum | solution.py:104
  80.5 0.0 all-to-all-done.1
  80.5 1.5 %fusion.6 = f32[8,32,256]{2,0,1:T(8,128)S(1)} fusion(f32[8,4,32,256]{3,2,1,0:T(8,128)S(1)} %bitcast.96, f32[256]{0:T(256)S(1)} %psum.7, f32[8]{0:T(128)S(1)} %dynamic_slice.23, s32[8,8]{1,0:T(8,128)S(1)} %bitcast_subtract_fusion), kind=kOutput, calls=%fused_computation.21 | convolution fusion | flops 25297152 | bytes 1312032 | tf_op jit(solution)/shard_map/jas,asrv->jrv/dot_general | solution.py:129
  82.0 0.8 copy.78
  (11 shorter events, 0.1 us)
Async XLA Ops:
  2.3 9.0 %copy-start.1 = (bf16[1,32,11264]{2,1,0:T(8,128)(2,1)S(1)}, bf16[1,32,11264]{2,1,0:T(8,128)(2,1)}, u32[]{:S(2)}) copy-start(bf16[1,32,11264]{2,1,0:T(8,128)(2,1)} %param.5) | copy-start | bytes 2162692
  4.9 10.3 %copy-start.2 = (bf16[1,256,256]{2,1,0:T(8,128)(2,1)S(1)}, bf16[1,256,256]{2,1,0:T(8,128)(2,1)}, u32[]{:S(2)}) copy-start(bf16[1,256,256]{2,1,0:T(8,128)(2,1)} %param.7) | copy-start | bytes 393220
  4.9 19.6 %all-to-all-start = ((bf16[8,4,32,256]{3,2,1,0:T(8,128)(2,1)}), bf16[8,4,32,256]{3,2,1,0:T(8,128)(2,1)S(1)}, u32[]{:S(2)}, u32[]{:S(2)}) async-start(bf16[8,4,32,256]{3,2,1,0:T(8,128)(2,1)} %copy.72), calls=%async_computation | async-start | bytes 1048576 | tf_op jit(solution)/shard_map/all_to_all | solution.py:115
  11.4 6.3 %collective-permute-start = (bf16[1,3,11264]{2,1,0:T(4,128)(2,1)S(1)}, bf16[1,3,11264]{2,1,0:T(4,128)(2,1)S(1)}, u32[]{:S(2)}, u32[]{:S(2)}) collective-permute-start(bf16[1,3,11264]{2,1,0:T(4,128)(2,1)S(1)} %get-tuple-element.19), channel_id=1, source_target_pairs={{0,1},{1,2},{2,3},{4,5},{5,6},{6,7},{8,9},{9,10},{10,11},{12,13},{... | collective-permute-start | bytes 202760 | tf_op jit(solution)/shard_map/ppermute | solution.py:18
  12.7 4.9 %collective-permute-start.1 = (bf16[1,3,11264]{2,1,0:T(4,128)(2,1)S(1)}, bf16[1,3,11264]{2,1,0:T(4,128)(2,1)S(1)}, u32[]{:S(2)}, u32[]{:S(2)}) collective-permute-start(bf16[1,3,11264]{2,1,0:T(4,128)(2,1)S(1)} %get-tuple-element.18), channel_id=1, source_target_pairs={{1,0},{2,1},{3,2},{5,4},{6,5},{7,6},{9,8},{10,9},{11,10},{13,12},{... | collective-permute-start | bytes 202760 | tf_op jit(solution)/shard_map/ppermute | solution.py:21
  30.7 1.4 %copy-start = (f32[1,32,11264]{2,1,0:T(8,128)S(1)}, f32[1,32,11264]{2,1,0:T(8,128)}, u32[]{:S(2)}) copy-start(f32[1,32,11264]{2,1,0:T(8,128)} %multiply_add_fusion) | copy-start | bytes 4325380
  41.9 38.7 %all-to-all-start.1 = ((f32[1,32,32,256]{3,2,0,1:T(8,128)}), f32[1,32,32,256]{3,2,0,1:T(8,128)S(1)}, u32[]{:S(2)}, u32[]{:S(2)}) async-start(f32[1,32,32,256]{3,2,0,1:T(8,128)} %fusion.7), calls=%async_computation.1 | async-start | bytes 2097152 | tf_op jit(solution)/shard_map/all_to_all | solution.py:128
where the time goes:
time: 83.4 us; the launch traced here: 82.8 us
  blocking collectives  33.8 us (41%)
  starting transfers between devices  13.9 us (17%)
  other arithmetic  13.8 us (17%)
  local copies, waits for them, and re-layouts  9.5 us (11%)
  waiting for transfers between devices  6.21 us (7%)
  matrix products  4.79 us (6%)
  between operations  0.84 us (1%)
    psum x1, blocking collectives, local(): lax.psum(jnp.sum(footprint, axis=(0, 2), dtype=jnp.float32), 'tile')  33.8 us
    all_to_all x1, starting transfers between devices, local(): lax.all_to_all(outgoing.astype(jnp.bfloat16), 'tile', split_axis=0, conca...  6.41 us
    all_to_all x1, starting transfers between devices, local(): lax.all_to_all(returned, 'tile', split_axis=1, concat_axis=0, tiled=True)  4.9 us
    all_to_all x1, waiting for transfers between devices, local(): lax.all_to_all(outgoing.astype(jnp.bfloat16), 'tile', split_axis=0, conca...  4.39 us
    scatter-add x1, other arithmetic, local(): jax.ops.segment_sum(arrived[0], targets[0], num_segments=block_count)  3.78 us
    unnamed x1, other arithmetic  3.4 us
    add x1, other arithmetic, retrieve_phase(): across + float(tap_weights[tap_index]) * padded[:, tap_index:tap_index +...  2.47 us
    select_n x2, other arithmetic, local(): returned = jnp.stack([jnp.take(back_blocks[0], targets[0], axis=0)])  2.36 us
  transfers between devices with their start and end apart: 4, of which 2 were waited for; matrix products, arithmetic and copies ran while one was open for 5% of the time, Pallas kernels for 0%

commit v1 on v0

--- a/solution.py
+++ b/solution.py
@@ -101,7 +101,9 @@
     live_mine = lax.dynamic_slice_in_dim(live_all, member * slots_here, slots_here)
     masked = volume * live_mine[:, None, None]
     offsets_here = lax.dynamic_slice_in_dim(foot_offset, member * angles_here, angles_here, 1)
-    column_sums = lax.psum(jnp.sum(footprint, axis=(0, 2), dtype=jnp.float32), "tile")
+    column_sums = jnp.sum(
+        lax.all_gather(jnp.sum(footprint, axis=(0, 2), dtype=jnp.float32), "tile"), axis=0
+    )
     row_sums = row_totals(footprint, offsets_here, live_all, block_count)
     group_total = tile_count.shape[0]
     grouped = foot_offset.reshape(group_total, slots_here, -1)

time: 83.4 us -> 83.2 us (level)
    psum x1 -> x0, blocking collectives: 33.8 us -> none  [local(): lax.psum(jnp.sum(footprint, axis=(0, 2), dtype=jnp.float32), 'tile')]
    all_gather x0 -> x1, blocking collectives: none -> 33.5 us  [local(): lax.all_gather(jnp.sum(footprint, axis=(0, 2), dtype=jnp.float32), 'tile')]
where the time goes in v1:
time: 83.2 us; the launch traced here: 82.6 us
  blocking collectives  33.5 us (40%)
  starting transfers between devices  13.9 us (17%)
  other arithmetic  13.8 us (17%)
  local copies, waits for them, and re-layouts  9.5 us (11%)
  waiting for transfers between devices  6.21 us (7%)
  matrix products  4.79 us (6%)
  between operations  0.84 us (1%)
    all_gather x1, blocking collectives, local(): lax.all_gather(jnp.sum(footprint, axis=(0, 2), dtype=jnp.float32), 'tile')  33.5 us
    all_to_all x1, starting transfers between devices, local(): lax.all_to_all(outgoing.astype(jnp.bfloat16), 'tile', split_axis=0, conca...  6.41 us
    all_to_all x1, starting transfers between devices, local(): lax.all_to_all(returned, 'tile', split_axis=1, concat_axis=0, tiled=True)  4.9 us
    all_to_all x1, waiting for transfers between devices, local(): lax.all_to_all(outgoing.astype(jnp.bfloat16), 'tile', split_axis=0, conca...  4.39 us
    scatter-add x1, other arithmetic, local(): jax.ops.segment_sum(arrived[0], targets[0], num_segments=block_count)  3.78 us
    unnamed x1, other arithmetic  3.4 us
    add x1, other arithmetic, retrieve_phase(): across + float(tap_weights[tap_index]) * padded[:, tap_index:tap_index +...  2.47 us
    select_n x2, other arithmetic, local(): returned = jnp.stack([jnp.take(back_blocks[0], targets[0], axis=0)])  2.36 us
  transfers between devices with their start and end apart: 4, of which 2 were waited for; matrix products, arithmetic and copies ran while one was open for 5% of the time, Pallas kernels for 0%

profile of v1, /device:TPU:8, one launch (start us, length us, event | category | flops | bytes accessed | tf_op | source)
XLA Modules:
  0.0 82.6 jit_solution(4081496611962584144)
XLA Ops:
  0.6 0.7 broadcast_in_dim.12
  1.4 0.1 reshape.331
  1.4 0.8 copy.69
  2.2 0.1 dynamic_slice.23
  2.3 0.0 copy-start.1
  2.3 1.7 %convolution_convert_fusion = bf16[8,4,32,256]{3,0,2,1:T(8,128)(2,1)S(1)} fusion(f32[8,32,256]{2,1,0:T(8,128)} %param.6, f32[8]{0:T(128)S(1)} %dynamic_slice.23, s32[8,8]{1,0:T(8,128)S(1)} %bitcast_subtract_fusion), kind=kOutput, calls=%fused_computation.16 | convolution fusion | flops 25493760 | bytes 786720 | tf_op jit(solution)/shard_map/jas,jrv->asrv/dot_general | solution.py:116
  4.0 0.9 %copy.72 = bf16[8,4,32,256]{3,2,1,0:T(8,128)(2,1)} copy(bf16[8,4,32,256]{3,0,2,1:T(8,128)(2,1)S(1)} %convolution_convert_fusion) | data formatting | bytes 1048576 | tf_op jit(solution)/shard_map/convert_element_type | solution.py:118
  4.9 0.0 copy-start.2
  4.9 6.4 %all-to-all-start = ((bf16[8,4,32,256]{3,2,1,0:T(8,128)(2,1)}), bf16[8,4,32,256]{3,2,1,0:T(8,128)(2,1)S(1)}, u32[]{:S(2)}, u32[]{:S(2)}) async-start(bf16[8,4,32,256]{3,2,1,0:T(8,128)(2,1)} %copy.72), calls=%async_computation | async-start | bytes 1048576 | tf_op jit(solution)/shard_map/all_to_all | solution.py:117
  11.3 0.0 copy-done.1
  11.3 0.1 fusion.28
  11.4 1.3 %collective-permute-start = (bf16[1,3,11264]{2,1,0:T(4,128)(2,1)S(1)}, bf16[1,3,11264]{2,1,0:T(4,128)(2,1)S(1)}, u32[]{:S(2)}, u32[]{:S(2)}) collective-permute-start(bf16[1,3,11264]{2,1,0:T(4,128)(2,1)S(1)} %get-tuple-element.19), channel_id=1, source_target_pairs={{0,1},{1,2},{2,3},{4,5},{5,6},{6,7},{8,9},{9,10},{10,11},{12,13},{... | collective-permute-start | bytes 202760 | tf_op jit(solution)/shard_map/ppermute | solution.py:18
  12.7 1.3 %collective-permute-start.1 = (bf16[1,3,11264]{2,1,0:T(4,128)(2,1)S(1)}, bf16[1,3,11264]{2,1,0:T(4,128)(2,1)S(1)}, u32[]{:S(2)}, u32[]{:S(2)}) collective-permute-start(bf16[1,3,11264]{2,1,0:T(4,128)(2,1)S(1)} %get-tuple-element.18), channel_id=1, source_target_pairs={{1,0},{2,1},{3,2},{5,4},{6,5},{7,6},{9,8},{10,9},{11,10},{13,12},{... | collective-permute-start | bytes 202760 | tf_op jit(solution)/shard_map/ppermute | solution.py:21
  14.0 0.7 fusion.26
  14.7 0.2 dynamic-slice_reduce_fusion
  14.9 0.1 add.149
  15.0 0.1 add.150
  15.1 0.1 add.157
  15.2 0.0 copy-done.2
  15.2 0.1 convert_reduce_fusion
  15.3 0.1 select_reduce_fusion
  15.4 0.1 add.152
  15.5 0.1 add.159
  15.6 0.1 broadcast_multiply_fusion
  15.7 0.1 maximum_bitcast_fusion
  15.8 1.8 %collective-permute-done.1 = bf16[1,3,11264]{2,1,0:T(4,128)(2,1)S(1)} collective-permute-done((bf16[1,3,11264]{2,1,0:T(4,128)(2,1)S(1)}, bf16[1,3,11264]{2,1,0:T(4,128)(2,1)S(1)}, u32[]{:S(2)}, u32[]{:S(2)}) %collective-permute-start.1) | collective-permute-done | bytes 67616 | tf_op jit(solution)/shard_map/ppermute | solution.py:21
  17.6 0.1 constant_dynamic-update-slice_fusion
  17.7 0.0 collective-permute-done
  17.7 2.5 %multiply_add_fusion = f32[1,32,11264]{2,1,0:T(8,128)} fusion(bf16[1,32,11264]{2,1,0:T(8,128)(2,1)S(1)} %copy-done.1, bf16[1,3,11264]{2,1,0:T(4,128)(2,1)S(1)} %collective-permute-done, bf16[1,35,11264]{2,1,0:T(8,128)(2,1)S(1)} %constant_dynamic-update-slice_fusion), kind=kLoop, calls=%fused_computation.15 | loop fusion | flops 10452992 | bytes 4392960 | tf_op jit(solution)/shard_map/add | solution.py:38
  20.2 4.4 %all-to-all-done = bf16[8,4,32,256]{3,2,1,0:T(8,128)(2,1)S(1)} async-done(((bf16[8,4,32,256]{3,2,1,0:T(8,128)(2,1)}), bf16[8,4,32,256]{3,2,1,0:T(8,128)(2,1)S(1)}, u32[]{:S(2)}, u32[]{:S(2)}) %all-to-all-start) | async-done | bytes 524320 | tf_op jit(solution)/shard_map/all_to_all | solution.py:117
  24.6 1.1 %bitcast_convert_fusion = f32[32,32,256]{2,1,0:T(8,128)} fusion(bf16[8,4,32,256]{3,2,1,0:T(8,128)(2,1)S(1)} %all-to-all-done), kind=kLoop, calls=%fused_computation.31 | loop fusion | flops 262144 | bytes 1572864 | tf_op jit(solution)/shard_map/convert_element_type | solution.py:119
  25.7 0.3 broadcast_in_dim.11
  26.0 3.8 %scatter_fusion = f32[88,32,256]{2,1,0:T(8,128)S(1)} fusion(f32[88,32,256]{2,1,0:T(8,128)S(1)} %broadcast_in_dim.11, s32[32]{0:T(128)S(1)} %get-tuple-element.21, f32[32,32,256]{2,1,0:T(8,128)} %bitcast_convert_fusion), kind=kCustom, calls=%fused_computation.1 | custom fusion | flops 262144 | bytes 3145856 | tf_op jit(solution)/shard_map/scatter-add | solution.py:124
  29.8 0.5 convolution_bitcast_fusion.1
  30.4 0.1 slice.107
  30.5 0.2 slice_add_fusion
  30.7 0.0 copy-start
  30.8 0.8 %copy.73 = f32[1,32,88,128]{3,2,0,1:T(8,128)S(1)} copy(f32[1,32,88,128]{3,1,2,0:T(8,128)S(1)} %slice_add_fusion) | data formatting | bytes 2883584 | tf_op jit(solution)/shard_map/add | solution.py:76
  31.6 0.5 copy-done
  32.1 3.4 %fusion.11 = (bf16[4,8,88,128]{3,1,2,0:T(8,128)(2,1)S(1)}, f32[1,32,11264]{2,1,0:T(8,128)}) fusion(f32[11264]{0:T(1024)S(1)} %maximum_bitcast_fusion, f32[1,32,11264]{2,0,1:T(1,128)S(1)} %bitcast.96, f32[1,32,11264]{2,1,0:T(8,128)S(1)} %copy-done), kind=kLoop, calls=%fused_computation.30 | loop fusion | flops 6127616 | bytes 5091328
  35.5 0.1 copy.83
  35.6 0.6 convolution_bitcast_fusion
  36.2 0.2 slice.111
  36.4 0.6 fusion
  37.0 0.9 %copy.75 = f32[88,32,256]{2,1,0:T(8,128)S(1)} copy(f32[88,32,256]{2,0,1:T(8,128)S(1)} %fusion) | data formatting | bytes 5767168 | tf_op jit(solution)/shard_map/squeeze | solution.py:129
  37.9 1.6 %gather_fusion = f32[32,32,256]{2,1,0:T(8,128)} fusion(f32[88,32,256]{2,1,0:T(8,128)S(1)} %copy.75, s32[1024]{0:T(1024)S(1)} %pad_clamp_fusion), kind=kCustom, calls=%fused_computation | custom fusion | bytes 2097280 | tf_op jit(solution)/shard_map/jit(_take)/gather | solution.py:129
  39.5 2.4 %fusion.7 = f32[1,32,32,256]{3,2,0,1:T(8,128)} fusion(f32[32,32,256]{2,1,0:T(8,128)} %gather_fusion, pred[32]{0:T(512)(128)(4,1)S(1)} %compare_and_fusion), kind=kLoop, calls=%fused_computation.23 | loop fusion | flops 262144 | bytes 2097184 | tf_op jit(solution)/shard_map/jit(_take)/select_n | solution.py:129
  41.9 4.9 %all-to-all-start.1 = ((f32[1,32,32,256]{3,2,0,1:T(8,128)}), f32[1,32,32,256]{3,2,0,1:T(8,128)S(1)}, u32[]{:S(2)}, u32[]{:S(2)}) async-start(f32[1,32,32,256]{3,2,0,1:T(8,128)} %fusion.7), calls=%async_computation.1 | async-start | bytes 2097152 | tf_op jit(solution)/shard_map/all_to_all | solution.py:130
  46.8 33.5 %all-gather.1 = f32[8,1,256]{2,1,0:T(1,128)S(1)} all-gather(f32[1,1,256]{2,1,0:T(1,128)S(1)} %bitcast.99), channel_id=2, replica_groups=mesh['tile'=8,'row'=4] {'tile'}, dimensions={0}, use_global_device_ids=true | all-gather | bytes 9216 | tf_op jit(solution)/shard_map/all_gather | solution.py:105
  80.3 0.0 all-to-all-done.1
  80.3 1.5 %fusion.6 = f32[8,32,256]{2,0,1:T(8,128)S(1)} fusion(f32[8,4,32,256]{3,2,1,0:T(8,128)S(1)} %bitcast.97, f32[256]{0:T(256)S(1)} %reduce_sum.42, f32[8]{0:T(128)S(1)} %dynamic_slice.23, s32[8,8]{1,0:T(8,128)S(1)} %bitcast_subtract_fusion), kind=kOutput, calls=%fused_computation.21 | convolution fusion | flops 25297152 | bytes 1312032 | tf_op jit(solution)/shard_map/jas,asrv->jrv/dot_general | solution.py:131
  81.8 0.8 copy.78
  (12 shorter events, 0.1 us)
Async XLA Ops:
  2.3 9.0 %copy-start.1 = (bf16[1,32,11264]{2,1,0:T(8,128)(2,1)S(1)}, bf16[1,32,11264]{2,1,0:T(8,128)(2,1)}, u32[]{:S(2)}) copy-start(bf16[1,32,11264]{2,1,0:T(8,128)(2,1)} %param.5) | copy-start | bytes 2162692
  4.9 10.3 %copy-start.2 = (bf16[1,256,256]{2,1,0:T(8,128)(2,1)S(1)}, bf16[1,256,256]{2,1,0:T(8,128)(2,1)}, u32[]{:S(2)}) copy-start(bf16[1,256,256]{2,1,0:T(8,128)(2,1)} %param.7) | copy-start | bytes 393220
  4.9 19.6 %all-to-all-start = ((bf16[8,4,32,256]{3,2,1,0:T(8,128)(2,1)}), bf16[8,4,32,256]{3,2,1,0:T(8,128)(2,1)S(1)}, u32[]{:S(2)}, u32[]{:S(2)}) async-start(bf16[8,4,32,256]{3,2,1,0:T(8,128)(2,1)} %copy.72), calls=%async_computation | async-start | bytes 1048576 | tf_op jit(solution)/shard_map/all_to_all | solution.py:117
  11.4 6.3 %collective-permute-start = (bf16[1,3,11264]{2,1,0:T(4,128)(2,1)S(1)}, bf16[1,3,11264]{2,1,0:T(4,128)(2,1)S(1)}, u32[]{:S(2)}, u32[]{:S(2)}) collective-permute-start(bf16[1,3,11264]{2,1,0:T(4,128)(2,1)S(1)} %get-tuple-element.19), channel_id=1, source_target_pairs={{0,1},{1,2},{2,3},{4,5},{5,6},{6,7},{8,9},{9,10},{10,11},{12,13},{... | collective-permute-start | bytes 202760 | tf_op jit(solution)/shard_map/ppermute | solution.py:18
  12.7 4.9 %collective-permute-start.1 = (bf16[1,3,11264]{2,1,0:T(4,128)(2,1)S(1)}, bf16[1,3,11264]{2,1,0:T(4,128)(2,1)S(1)}, u32[]{:S(2)}, u32[]{:S(2)}) collective-permute-start(bf16[1,3,11264]{2,1,0:T(4,128)(2,1)S(1)} %get-tuple-element.18), channel_id=1, source_target_pairs={{1,0},{2,1},{3,2},{5,4},{6,5},{7,6},{9,8},{10,9},{11,10},{13,12},{... | collective-permute-start | bytes 202760 | tf_op jit(solution)/shard_map/ppermute | solution.py:21
  30.7 1.4 %copy-start = (f32[1,32,11264]{2,1,0:T(8,128)S(1)}, f32[1,32,11264]{2,1,0:T(8,128)}, u32[]{:S(2)}) copy-start(f32[1,32,11264]{2,1,0:T(8,128)} %multiply_add_fusion) | copy-start | bytes 4325380
  41.9 38.5 %all-to-all-start.1 = ((f32[1,32,32,256]{3,2,0,1:T(8,128)}), f32[1,32,32,256]{3,2,0,1:T(8,128)S(1)}, u32[]{:S(2)}, u32[]{:S(2)}) async-start(f32[1,32,32,256]{3,2,0,1:T(8,128)} %fusion.7), calls=%async_computation.1 | async-start | bytes 2097152 | tf_op jit(solution)/shard_map/all_to_all | solution.py:130
